TPU v7x, 32 devices: a whole 2x2x4 slice. The times are simulated.
32 devices in a mesh: dp: 2 (over core), space: 16 (over z, y, x).
Axes of the slice: x: 2, y: 2, z: 4, core: 2. Of those that a mesh axis runs over, the one named last changes fastest.
Arguments:
- master: float32 [1156352], P(('dp', 'space')), may hold values from -0.375 to 0.375
- moment1: float32 [1156352], P(('dp', 'space')), may hold values from -7.6293945e-05 to 7.6293945e-05
- moment2: float32 [1156352], P(('dp', 'space')), may hold values from 2.1619713e-12 to 8.647885e-12
- inputs: bfloat16 [2, 78, 8192], P('dp', None, 'space'), may hold values from -6 to 6
- targets: bfloat16 [2, 78, 8192], P('dp', None, 'space'), may hold values from -6 to 6
- valid: int32 [2, 78, 8192], P('dp', None, 'space'), may hold values from 0 to 1
- owner: int32 [2, 8192, 1], P('dp', 'space'), may hold values from 0 to 15; in each aligned block of 512 rows (0 to 511, 512 to 1023, ..., all dimensions but the last counted through in order) at most 64 rows name the same one
- slot: int32 [2, 8192], P('dp', 'space'), may hold values from 0 to 2047
- neighbours: int32 [32768, 6], P('space'), may hold values from 0 to 32767, as said below
- partner: int32 [8192], P('space'), may hold values from 0 to 8191, as said below
Outputs:
- loss_total: float32 [1], replicated
- valid_count: float32 [1], replicated
- grad_norm: float32 [1], replicated
- new_master: float32 [1156352], P(('dp', 'space'))
- new_moment1: float32 [1156352], P(('dp', 'space'))
- new_moment2: float32 [1156352], P(('dp', 'space'))
- new_copy: bfloat16 [1156352], P(('dp', 'space'))
- final_mesh: float32 [2, 32768, 256], P('dp', 'space')
- node_grads: float32 [2, 32768, 256], P('dp', 'space')
- pred_grads: float32 [2, 78, 8192], P('dp', None, 'space')
Inputs may be any that keep to these rules, and one draw needn't show every extreme that they name: `neighbours`: each entry is a node number within 2048 of its row's own number, counted cyclically over 32768; a distance of exactly 2048 occurs in both directions. partner[g] - g lies in 358 to 360; where that passes the last point, partner[g] = g.
All inputs are finite; a program needn't handle non-finite values.
Results may differ from a plain program's by a relative error of at most 0.014.
Values may be sent and summed in bfloat16 or wider, within the bound.
No kernel may reach another device: no remote copies, remote signals or barrier semaphores. Data moves between devices by JAX's collectives and lax.ppermute only.
A program may use at most 192 MiB of HBM per device.

v0:
```python
import math
import jax
import jax.numpy as jnp
from jax import lax
from jax.sharding import PartitionSpec as P

D = 256
CH = 78
ROUNDS = 3
K = 6
ROWW = 360
STEP = 10
H = 2048


def extended(shard, sides, width):
    for axis, dim in sides:
        peers, length = (lax.axis_size(axis), shard.shape[dim])
        up = [(i, (i + 1) % peers) for i in range(peers)]
        down = [(j, i) for i, j in up]
        last = lax.slice_in_dim(shard, length - width, length, axis=dim)
        initial = lax.slice_in_dim(shard, 0, width, axis=dim)
        before = lax.ppermute(last, axis, up)
        after = lax.ppermute(initial, axis, down)
        shard = jnp.concatenate([before, shard, after], axis=dim)
    return shard


def shifted(shard, axis, by):
    peers = lax.axis_size(axis)
    pairs = [(i, i + by) for i in range(peers) if 0 <= i + by < peers]
    return lax.ppermute(shard, axis, pairs)


def layout():
    return [(CH, D), (D, D), (D, D), (D, CH), (ROUNDS, 5, D, D), (3, D), (ROUNDS, 2, D)]


def unpack(flat):
    pieces = []
    start = 0
    for shape in layout():
        count = math.prod(shape)
        pieces.append(flat[start : start + count].reshape(shape))
        start = start + count
    return pieces


def inner(left, right, left_dim, right_dim):
    return lax.dot_general(
        left, right, (((left_dim,), (right_dim,)), ((), ())), preferred_element_type=jnp.float32
    )


def slope(value):
    sigma = jax.nn.sigmoid(value)
    return sigma * (1.0 + value * (1.0 - sigma))


def edge_inputs(padded, dest, places, edge):
    return padded[places[:, edge]].astype(jnp.float32) + dest


def round_forward(mesh, mats, bias, places):
    lowered = mesh.astype(jnp.bfloat16)
    sent = inner(lowered, mats[0], 1, 0).astype(jnp.bfloat16)
    padded = extended(sent, (("space", 0),), H)
    dest = inner(lowered, mats[1], 1, 0) + bias[0]
    agg = jnp.zeros_like(mesh)
    for edge in range(K):
        agg = agg + jax.nn.silu(edge_inputs(padded, dest, places, edge))
    agg = agg / K
    update_in = (
        inner(agg.astype(jnp.bfloat16), mats[2], 1, 0) + inner(lowered, mats[3], 1, 0) + bias[1]
    )
    update = jax.nn.silu(update_in).astype(jnp.bfloat16)
    return (mesh + inner(update, mats[4], 1, 0), padded)


def round_backward(grad_mesh, mesh, padded, mats, bias, places):
    blocks = mesh.shape[0]
    lowered = mesh.astype(jnp.bfloat16)
    dest = inner(lowered, mats[1], 1, 0) + bias[0]
    agg = jnp.zeros_like(mesh)
    for edge in range(K):
        agg = agg + jax.nn.silu(edge_inputs(padded, dest, places, edge))
    agg = agg / K
    agg_low = agg.astype(jnp.bfloat16)
    update_in = inner(agg_low, mats[2], 1, 0) + inner(lowered, mats[3], 1, 0) + bias[1]
    update = jax.nn.silu(update_in).astype(jnp.bfloat16)
    grad_out = grad_mesh.astype(jnp.bfloat16)
    grad_final = inner(update, grad_out, 0, 0)
    grad_update = inner(grad_out, mats[4], 1, 1)
    grad_uin = (grad_update * slope(update_in)).astype(jnp.bfloat16)
    grad_bupd = jnp.sum(grad_uin.astype(jnp.float32), 0)
    grad_aggw = inner(agg_low, grad_uin, 0, 0)
    grad_selfw = inner(lowered, grad_uin, 0, 0)
    grad_agg = inner(grad_uin, mats[2], 1, 1) / K
    grad_low = inner(grad_uin, mats[3], 1, 1)
    grad_pad = jnp.zeros((padded.shape[0], mesh.shape[1]), jnp.float32)
    grad_dest = jnp.zeros_like(mesh)
    for edge in range(K):
        grad_edge = grad_agg * slope(edge_inputs(padded, dest, places, edge))
        grad_dest = grad_dest + grad_edge
        grad_pad = grad_pad.at[places[:, edge]].add(grad_edge)
    dest_low = grad_dest.astype(jnp.bfloat16)
    grad_bedge = jnp.sum(dest_low.astype(jnp.float32), 0)
    grad_dstw = inner(lowered, dest_low, 0, 0)
    grad_low = grad_low + inner(dest_low, mats[1], 1, 1)
    edges = jnp.concatenate([grad_pad[:H], grad_pad[blocks + H :]], 0)
    widened = extended(edges.astype(jnp.bfloat16), (("space", 0),), H).astype(edges.dtype)
    grad_sent = grad_pad[H : H + blocks]
    grad_sent = grad_sent.at[:H].add(widened[:H]).at[blocks - H :].add(widened[3 * H :])
    sent_low = grad_sent.astype(jnp.bfloat16)
    grad_srcw = inner(lowered, sent_low, 0, 0)
    grad_low = grad_low + inner(sent_low, mats[0], 1, 1)
    mats_grad = jnp.stack([grad_srcw, grad_dstw, grad_aggw, grad_selfw, grad_final])
    return (grad_mesh + grad_low, mats_grad, jnp.stack([grad_bedge, grad_bupd]))


def shards(master, moment1, moment2, inputs, targets, valid, owner, slot, neighbours, partner):
    bands = lax.axis_size("space")
    band = lax.axis_index("space")
    shard = master.shape[0]
    everything = lax.all_gather(master.astype(jnp.bfloat16), ("dp", "space"), axis=0, tiled=True)
    w_in, w_node, w_dec, w_out, w_round, b_head, b_round = unpack(everything)
    state_in = inputs[0]
    wanted = targets[0].astype(jnp.float32)
    counted = valid[0].astype(jnp.float32)
    points = state_in.shape[1]
    blocks = neighbours.shape[0]
    capacity = max(2, 2 * points // bands)
    target_band = owner[0, :, 0]
    hits = (target_band[:, None] == jnp.arange(bands, dtype=jnp.int32)[None, :]).astype(jnp.int32)
    ranks = jnp.sum(jnp.cumsum(hits, 0) * hits, 1) - 1
    places_out = target_band * capacity + ranks
    enc_in = inner(state_in, w_in, 0, 0) + b_head[0]
    encoded = jax.nn.silu(enc_in).astype(jnp.bfloat16)
    outbox = jnp.zeros((bands * capacity, D), jnp.bfloat16).at[places_out].set(encoded)
    labels = jnp.full((bands * capacity,), -1, jnp.int32).at[places_out].set(slot[0])
    arrived, arrived_ids = (
        lax.all_to_all(
            outbox.reshape(bands, capacity, D), "space", split_axis=0, concat_axis=0, tiled=True
        ),
        lax.all_to_all(
            labels.reshape(bands, capacity), "space", split_axis=0, concat_axis=0, tiled=True
        ),
    )
    chooser = (
        arrived_ids.reshape(-1)[:, None] == jnp.arange(blocks, dtype=jnp.int32)[None, :]
    ).astype(jnp.bfloat16)
    gathered = inner(chooser, arrived.reshape(-1, D), 0, 0).astype(jnp.bfloat16)
    node_in = inner(gathered, w_node, 1, 0) + b_head[1]
    mesh = jax.nn.silu(node_in)
    places = (neighbours - band * blocks + H) % (blocks * bands)
    kept_mesh = []
    kept_pad = []
    for layer in range(ROUNDS):
        kept_mesh.append(mesh)
        mesh, padded = round_forward(mesh, w_round[layer], b_round[layer], places)
        kept_pad.append(padded)
    reply = inner(chooser, mesh.astype(jnp.bfloat16), 1, 0).astype(jnp.bfloat16)
    returned = lax.all_to_all(
        reply.reshape(bands, capacity, D), "space", split_axis=0, concat_axis=0, tiled=True
    )
    fetched = returned.reshape(-1, D)[places_out]
    dec_in = inner(fetched, w_dec, 1, 0) + b_head[2]
    decoded = jax.nn.silu(dec_in).astype(jnp.bfloat16)
    err = state_in.astype(jnp.float32) + inner(w_out, decoded, 0, 1) - wanted
    head_err, head_valid = (
        shifted(err[:, :ROWW].astype(jnp.bfloat16), "space", -1).astype(jnp.float32),
        shifted(counted[:, :ROWW].astype(jnp.bfloat16), "space", -1).astype(jnp.float32),
    )
    wide_err = jnp.concatenate([err, head_err], 1)
    wide_valid = jnp.concatenate([counted, head_valid], 1)
    partner_at = partner - band * points
    err_far = wide_err[:, partner_at]
    valid_far = wide_valid[:, partner_at]
    gap = err - err_far
    local_total = jnp.sum(counted * err * err) + 0.5 * jnp.sum(counted * valid_far * gap * gap)
    total, count = lax.psum((local_total, jnp.sum(counted)), ("dp", "space"))
    paired = counted * valid_far * gap / count
    grad_err = 2.0 * counted * err / count + paired
    grad_wide = jnp.zeros(wide_err.shape, jnp.float32).at[:, partner_at].add(-paired)
    carried = shifted(grad_wide[:, points:].astype(jnp.bfloat16), "space", 1).astype(jnp.float32)
    grad_pred = (grad_err + grad_wide[:, :points]).at[:, :ROWW].add(carried)
    grad_branch = grad_pred.astype(jnp.bfloat16)
    grad_wout = inner(decoded, grad_branch, 0, 1)
    grad_dec = (inner(grad_branch, w_out, 0, 1) * slope(dec_in)).astype(jnp.bfloat16)
    grad_bdec = jnp.sum(grad_dec.astype(jnp.float32), 0)
    grad_wdec = inner(fetched, grad_dec, 0, 0)
    grad_fetched = inner(grad_dec, w_dec, 1, 1).astype(jnp.bfloat16)
    backbox = jnp.zeros((bands * capacity, D), jnp.bfloat16).at[places_out].set(grad_fetched)
    landed = lax.all_to_all(
        backbox.reshape(bands, capacity, D), "space", split_axis=0, concat_axis=0, tiled=True
    )
    grad_mesh = inner(chooser, landed.reshape(-1, D), 0, 0)
    mats_grads = []
    bias_grads = []
    for layer in reversed(range(ROUNDS)):
        grad_mesh, mats_grad, bias_grad = round_backward(
            grad_mesh, kept_mesh[layer], kept_pad[layer], w_round[layer], b_round[layer], places
        )
        mats_grads.insert(0, mats_grad)
        bias_grads.insert(0, bias_grad)
    grad_node = (grad_mesh * slope(node_in)).astype(jnp.bfloat16)
    grad_bnode = jnp.sum(grad_node.astype(jnp.float32), 0)
    grad_wnode = inner(gathered, grad_node, 0, 0)
    grad_gathered = inner(grad_node, w_node, 1, 1).astype(jnp.bfloat16)
    sendback = inner(chooser, grad_gathered, 1, 0).astype(jnp.bfloat16)
    homeward = lax.all_to_all(
        sendback.reshape(bands, capacity, D), "space", split_axis=0, concat_axis=0, tiled=True
    )
    grad_encoded = homeward.reshape(-1, D)[places_out].astype(jnp.float32)
    grad_enc = (grad_encoded * slope(enc_in)).astype(jnp.bfloat16)
    grad_bin = jnp.sum(grad_enc.astype(jnp.float32), 0)
    grad_win = inner(state_in, grad_enc, 1, 0)
    pieces = [
        grad_win,
        grad_wnode,
        grad_wdec,
        grad_wout,
        jnp.stack(mats_grads),
        jnp.stack([grad_bin, grad_bnode, grad_bdec]),
        jnp.stack(bias_grads),
    ]
    flat = jnp.concatenate([piece.reshape(-1) for piece in pieces])
    flat = jnp.concatenate([flat, jnp.zeros((everything.shape[0] - flat.shape[0],), jnp.float32)])
    summed = lax.psum(flat, ("dp", "space"))
    norm = jnp.sqrt(jnp.sum(summed * summed))
    mine = lax.dynamic_slice_in_dim(summed, lax.axis_index(("dp", "space")) * shard, shard)
    clipped = mine * jnp.minimum(1.0, 0.05 / norm)
    first = 0.9 * moment1 + 0.1 * clipped
    second = 0.999 * moment2 + 0.001 * clipped * clipped
    first_hat = first / (1.0 - 0.9**STEP)
    second_hat = second / (1.0 - 0.999**STEP)
    updated = master - 0.1 * (first_hat / (jnp.sqrt(second_hat) + 1e-08) + 0.1 * master)
    return (
        total.reshape(1),
        count.reshape(1),
        norm.reshape(1),
        updated,
        first,
        second,
        updated.astype(jnp.bfloat16),
        mesh.reshape(1, blocks, D),
        grad_mesh.reshape(1, blocks, D),
        grad_pred.reshape(1, grad_pred.shape[0], points),
    )


def solution(mesh):
    return jax.shard_map(
        shards,
        mesh=mesh,
        in_specs=(
            P(("dp", "space")),
            P(("dp", "space")),
            P(("dp", "space")),
            P("dp", None, "space"),
            P("dp", None, "space"),
            P("dp", None, "space"),
            P("dp", "space", None),
            P("dp", "space"),
            P("space", None),
            P("space"),
        ),
        out_specs=(
            P(),
            P(),
            P(),
            P(("dp", "space")),
            P(("dp", "space")),
            P(("dp", "space")),
            P(("dp", "space")),
            P("dp", "space", None),
            P("dp", "space", None),
            P("dp", None, "space"),
        ),
        check_vma=False,
    )
```

profile of v0, /device:TPU:0, one launch (start us, length us, event | category | flops | bytes accessed | tf_op | source)
XLA Modules:
  0.0 1434.8 jit_solution(12356482560449952227)
XLA Ops:
  32.4 118.8 %all-reduce.7.cloned.1.call-done = bf16[1156352]{0:T(1024)(128)(2,1)} async-done(((bf16[1156352]{0:T(1024)(128)(2,1)}), bf16[1156352]{0:T(1024)(128)(2,1)}) %all-reduce.7.cloned.1.call-update) | async-done | bytes 2312720
  164.6 12.9 all-to-all-done.1
  193.3 33.7 %collective-permute-done = bf16[2048,256]{1,0:T(8,128)(2,1)S(1)} collective-permute-done((bf16[2048,256]{1,0:T(8,128)(2,1)S(1)}, bf16[2048,256]{1,0:T(8,128)(2,1)S(1)}, u32[]{:S(2)}, u32[]{:S(2)}) %collective-permute-start) | collective-permute-done | bytes 1048608 | tf_op jit(solution)/shard_map/ppermute | solution.py:23
  231.2 9.0 gather_fusion.1
  240.2 9.7 gather_fusion.2
  249.9 9.7 gather_fusion.3
  259.6 9.7 gather_fusion.4
  269.4 9.7 gather_fusion.5
  311.6 35.0 %collective-permute-done.2 = bf16[2048,256]{1,0:T(8,128)(2,1)S(1)} collective-permute-done((bf16[2048,256]{1,0:T(8,128)(2,1)S(1)}, bf16[2048,256]{1,0:T(8,128)(2,1)S(1)}, u32[]{:S(2)}, u32[]{:S(2)}) %collective-permute-start.2) | collective-permute-done | bytes 1048608 | tf_op jit(solution)/shard_map/ppermute | solution.py:23
  356.2 9.7 gather_fusion.10
  365.9 9.7 gather_fusion.11
  375.6 9.0 gather_fusion.7
  384.6 9.7 gather_fusion.8
  394.4 9.7 gather_fusion.9
  404.1 9.0 gather_fusion.6
  435.2 38.1 %collective-permute-done.4 = bf16[2048,256]{1,0:T(8,128)(2,1)S(1)} collective-permute-done((bf16[2048,256]{1,0:T(8,128)(2,1)S(1)}, bf16[2048,256]{1,0:T(8,128)(2,1)S(1)}, u32[]{:S(2)}, u32[]{:S(2)}) %collective-permute-start.4) | collective-permute-done | bytes 1048608 | tf_op jit(solution)/shard_map/ppermute | solution.py:23
  477.5 9.0 gather_fusion.13
  486.5 9.9 gather_fusion.14
  496.4 9.0 gather_fusion.15
  505.4 9.9 gather_fusion.16
  524.2 9.0 gather_fusion.12
  593.9 47.1 %all-reduce.1 = (f32[1]{0:T(128)}, f32[]{:T(128)}) all-reduce(f32[1]{0:T(128)} %bitcast.23, f32[]{:T(128)} %fusion.67), channel_id=1, replica_groups=mesh['dp'=2,'space'=16] {'dp','space'}, use_global_device_ids=true, to_apply=%region_7.8 | all-reduce | flops 2 | bytes 16 | tf_op jit(solution)/shard_map/psum | solution.py:181
  676.6 12.4 all-to-all-done.3
  703.4 15.8 %scatter_custom_fusion.4 = f32[6144,256]{1,0:T(8,128)} fusion(s32[2048]{0:T(1024)} %bitcast.315, f32[]{:T(128)} %constant.352.clone.1, f32[2048,256]{1,0:T(8,128)} %get-tuple-element.236, f32[2048,256]{1,0:T(8,128)S(1)} %get-tuple-element.233, bf16[2048,256]{1,0:T(8,128)(2,1)} %gather_fusion.12), kind=kCustom, calls=%fused_computation.62 | custom fusion | flops 5767168 | bytes 11534848 | tf_op jit(solution)/shard_map/scatter-add | solution.py:105
  719.2 18.3 %scatter_custom_fusion.5 = f32[6144,256]{1,0:T(8,128)} fusion(f32[6144,256]{1,0:T(8,128)} %scatter_custom_fusion.4, s32[2048]{0:T(1024)} %bitcast.311, f32[2048,256]{1,0:T(8,128)} %get-tuple-element.236, f32[2048,256]{1,0:T(8,128)S(1)} %get-tuple-element.233, bf16[2048,256]{1,0:T(8,128)(2,1)} %gather_fusion.13), kind=kCustom, calls=%fused_computation.339 | custom fusion | flops 5767168 | bytes 11534336 | tf_op jit(solution)/shard_map/scatter-add | solution.py:105
  737.5 18.2 %scatter_custom_fusion.6 = f32[6144,256]{1,0:T(8,128)} fusion(f32[6144,256]{1,0:T(8,128)} %scatter_custom_fusion.5, s32[2048]{0:T(1024)} %bitcast.307, f32[2048,256]{1,0:T(8,128)} %get-tuple-element.236, f32[2048,256]{1,0:T(8,128)S(1)} %get-tuple-element.233, bf16[2048,256]{1,0:T(8,128)(2,1)} %gather_fusion.14), kind=kCustom, calls=%fused_computation.340 | custom fusion | flops 5767168 | bytes 11534336 | tf_op jit(solution)/shard_map/scatter-add | solution.py:105
  755.7 18.2 %scatter_custom_fusion.7 = f32[6144,256]{1,0:T(8,128)} fusion(f32[6144,256]{1,0:T(8,128)} %scatter_custom_fusion.6, s32[2048]{0:T(1024)} %bitcast.303, f32[2048,256]{1,0:T(8,128)} %get-tuple-element.236, f32[2048,256]{1,0:T(8,128)S(1)} %get-tuple-element.233, bf16[2048,256]{1,0:T(8,128)(2,1)} %gather_fusion.15), kind=kCustom, calls=%fused_computation.341 | custom fusion | flops 5767168 | bytes 11534336 | tf_op jit(solution)/shard_map/scatter-add | solution.py:105
  773.8 18.2 %scatter_custom_fusion.8 = f32[6144,256]{1,0:T(8,128)} fusion(f32[6144,256]{1,0:T(8,128)} %scatter_custom_fusion.7, s32[2048]{0:T(1024)} %bitcast.299, f32[2048,256]{1,0:T(8,128)} %get-tuple-element.236, f32[2048,256]{1,0:T(8,128)S(1)} %get-tuple-element.233, bf16[2048,256]{1,0:T(8,128)(2,1)} %gather_fusion.16), kind=kCustom, calls=%fused_computation.342 | custom fusion | flops 5767168 | bytes 11534336 | tf_op jit(solution)/shard_map/scatter-add | solution.py:105
  792.0 18.2 %scatter_custom_fusion.9 = f32[6144,256]{1,0:T(8,128)} fusion(f32[6144,256]{1,0:T(8,128)} %scatter_custom_fusion.8, s32[2048]{0:T(1024)} %bitcast.295, f32[2048,256]{1,0:T(8,128)} %get-tuple-element.236, f32[2048,256]{1,0:T(8,128)S(1)} %get-tuple-element.233, bf16[2048,256]{1,0:T(8,128)(2,1)} %gather_fusion.17), kind=kCustom, calls=%fused_computation.343 | custom fusion | flops 5767168 | bytes 11534336 | tf_op jit(solution)/shard_map/scatter-add | solution.py:105
  822.1 18.7 %collective-permute-done.10 = bf16[2048,256]{1,0:T(8,128)(2,1)} collective-permute-done((bf16[2048,256]{1,0:T(8,128)(2,1)}, bf16[2048,256]{1,0:T(8,128)(2,1)}, u32[]{:S(2)}, u32[]{:S(2)}) %collective-permute-start.10) | collective-permute-done | bytes 1048608 | tf_op jit(solution)/shard_map/ppermute | solution.py:24
  840.8 15.8 %collective-permute-done.9 = bf16[2048,256]{1,0:T(8,128)(2,1)} collective-permute-done((bf16[2048,256]{1,0:T(8,128)(2,1)S(1)}, bf16[2048,256]{1,0:T(8,128)(2,1)}, u32[]{:S(2)}, u32[]{:S(2)}) %collective-permute-start.9) | collective-permute-done | bytes 1048608 | tf_op jit(solution)/shard_map/ppermute | solution.py:23
  878.6 15.9 %scatter_custom_fusion.10 = f32[6144,256]{1,0:T(8,128)} fusion(s32[2048]{0:T(1024)} %bitcast.316, f32[]{:T(128)} %constant.352.clone.1, f32[2048,256]{1,0:T(8,128)} %get-tuple-element.237, f32[2048,256]{1,0:T(8,128)S(1)} %copy-done.1, bf16[2048,256]{1,0:T(8,128)(2,1)} %gather_fusion.6), kind=kCustom, calls=%fused_computation.60 | custom fusion | flops 5767168 | bytes 11534848 | tf_op jit(solution)/shard_map/scatter-add | solution.py:105
  894.5 18.2 %scatter_custom_fusion.11 = f32[6144,256]{1,0:T(8,128)} fusion(f32[6144,256]{1,0:T(8,128)} %scatter_custom_fusion.10, s32[2048]{0:T(1024)} %bitcast.312, f32[2048,256]{1,0:T(8,128)} %get-tuple-element.237, f32[2048,256]{1,0:T(8,128)S(1)} %copy-done.1, bf16[2048,256]{1,0:T(8,128)(2,1)} %gather_fusion.7), kind=kCustom, calls=%fused_computation.344 | custom fusion | flops 5767168 | bytes 11534336 | tf_op jit(solution)/shard_map/scatter-add | solution.py:105
  912.7 18.2 %scatter_custom_fusion.12 = f32[6144,256]{1,0:T(8,128)} fusion(f32[6144,256]{1,0:T(8,128)} %scatter_custom_fusion.11, s32[2048]{0:T(1024)} %bitcast.308, f32[2048,256]{1,0:T(8,128)} %get-tuple-element.237, f32[2048,256]{1,0:T(8,128)S(1)} %copy-done.1, bf16[2048,256]{1,0:T(8,128)(2,1)} %gather_fusion.8), kind=kCustom, calls=%fused_computation.345 | custom fusion | flops 5767168 | bytes 11534336 | tf_op jit(solution)/shard_map/scatter-add | solution.py:105
  930.8 18.2 %scatter_custom_fusion.13 = f32[6144,256]{1,0:T(8,128)} fusion(f32[6144,256]{1,0:T(8,128)} %scatter_custom_fusion.12, s32[2048]{0:T(1024)} %bitcast.304, f32[2048,256]{1,0:T(8,128)} %get-tuple-element.237, f32[2048,256]{1,0:T(8,128)S(1)} %copy-done.1, bf16[2048,256]{1,0:T(8,128)(2,1)} %gather_fusion.9), kind=kCustom, calls=%fused_computation.346 | custom fusion | flops 5767168 | bytes 11534336 | tf_op jit(solution)/shard_map/scatter-add | solution.py:105
  949.0 18.2 %scatter_custom_fusion.14 = f32[6144,256]{1,0:T(8,128)} fusion(f32[6144,256]{1,0:T(8,128)} %scatter_custom_fusion.13, s32[2048]{0:T(1024)} %bitcast.300, f32[2048,256]{1,0:T(8,128)} %get-tuple-element.237, f32[2048,256]{1,0:T(8,128)S(1)} %copy-done.1, bf16[2048,256]{1,0:T(8,128)(2,1)} %gather_fusion.10), kind=kCustom, calls=%fused_computation.347 | custom fusion | flops 5767168 | bytes 11534336 | tf_op jit(solution)/shard_map/scatter-add | solution.py:105
  967.1 18.2 %scatter_custom_fusion.15 = f32[6144,256]{1,0:T(8,128)} fusion(f32[6144,256]{1,0:T(8,128)} %scatter_custom_fusion.14, s32[2048]{0:T(1024)} %bitcast.296, f32[2048,256]{1,0:T(8,128)} %get-tuple-element.237, f32[2048,256]{1,0:T(8,128)S(1)} %copy-done.1, bf16[2048,256]{1,0:T(8,128)(2,1)} %gather_fusion.11), kind=kCustom, calls=%fused_computation.348 | custom fusion | flops 5767168 | bytes 11534336 | tf_op jit(solution)/shard_map/scatter-add | solution.py:105
  1000.3 36.0 %collective-permute-done.11 = bf16[2048,256]{1,0:T(8,128)(2,1)S(1)} collective-permute-done((bf16[2048,256]{1,0:T(8,128)(2,1)S(1)}, bf16[2048,256]{1,0:T(8,128)(2,1)S(1)}, u32[]{:S(2)}, u32[]{:S(2)}) %collective-permute-start.11) | collective-permute-done | bytes 1048608 | tf_op jit(solution)/shard_map/ppermute | solution.py:23
  1037.0 10.8 fusion.27
  1063.3 15.9 %scatter_custom_fusion.16 = f32[6144,256]{1,0:T(8,128)} fusion(s32[2048]{0:T(1024)} %bitcast.317, f32[]{:T(128)} %constant.352.clone.1, f32[2048,256]{1,0:T(8,128)} %get-tuple-element.238, f32[2048,256]{1,0:T(8,128)S(1)} %copy-done, bf16[2048,256]{1,0:T(8,128)(2,1)} %gather_fusion), kind=kCustom, calls=%fused_computation.58 | custom fusion | flops 5767168 | bytes 11534848 | tf_op jit(solution)/shard_map/scatter-add | solution.py:105
  1079.2 18.2 %scatter_custom_fusion.17 = f32[6144,256]{1,0:T(8,128)} fusion(f32[6144,256]{1,0:T(8,128)} %scatter_custom_fusion.16, s32[2048]{0:T(1024)} %bitcast.313, f32[2048,256]{1,0:T(8,128)} %get-tuple-element.238, f32[2048,256]{1,0:T(8,128)S(1)} %copy-done, bf16[2048,256]{1,0:T(8,128)(2,1)} %gather_fusion.1), kind=kCustom, calls=%fused_computation.349 | custom fusion | flops 5767168 | bytes 11534336 | tf_op jit(solution)/shard_map/scatter-add | solution.py:105
  1097.4 18.2 %scatter_custom_fusion.18 = f32[6144,256]{1,0:T(8,128)} fusion(f32[6144,256]{1,0:T(8,128)} %scatter_custom_fusion.17, s32[2048]{0:T(1024)} %bitcast.309, f32[2048,256]{1,0:T(8,128)} %get-tuple-element.238, f32[2048,256]{1,0:T(8,128)S(1)} %copy-done, bf16[2048,256]{1,0:T(8,128)(2,1)} %gather_fusion.2), kind=kCustom, calls=%fused_computation.350 | custom fusion | flops 5767168 | bytes 11534336 | tf_op jit(solution)/shard_map/scatter-add | solution.py:105
  1115.5 18.2 %scatter_custom_fusion.19 = f32[6144,256]{1,0:T(8,128)} fusion(f32[6144,256]{1,0:T(8,128)} %scatter_custom_fusion.18, s32[2048]{0:T(1024)} %bitcast.305, f32[2048,256]{1,0:T(8,128)} %get-tuple-element.238, f32[2048,256]{1,0:T(8,128)S(1)} %copy-done, bf16[2048,256]{1,0:T(8,128)(2,1)} %gather_fusion.3), kind=kCustom, calls=%fused_computation.351 | custom fusion | flops 5767168 | bytes 11534336 | tf_op jit(solution)/shard_map/scatter-add | solution.py:105
  1133.7 18.3 %scatter_custom_fusion.20 = f32[6144,256]{1,0:T(8,128)} fusion(f32[6144,256]{1,0:T(8,128)} %scatter_custom_fusion.19, s32[2048]{0:T(1024)} %bitcast.301, f32[2048,256]{1,0:T(8,128)} %get-tuple-element.238, f32[2048,256]{1,0:T(8,128)S(1)} %copy-done, bf16[2048,256]{1,0:T(8,128)(2,1)} %gather_fusion.4), kind=kCustom, calls=%fused_computation.352 | custom fusion | flops 5767168 | bytes 11534336 | tf_op jit(solution)/shard_map/scatter-add | solution.py:105
  1152.0 18.2 %scatter_custom_fusion.21 = f32[6144,256]{1,0:T(8,128)} fusion(f32[6144,256]{1,0:T(8,128)} %scatter_custom_fusion.20, s32[2048]{0:T(1024)} %bitcast.297, f32[2048,256]{1,0:T(8,128)} %get-tuple-element.238, f32[2048,256]{1,0:T(8,128)S(1)} %copy-done, bf16[2048,256]{1,0:T(8,128)(2,1)} %gather_fusion.5), kind=kCustom, calls=%fused_computation.353 | custom fusion | flops 5767168 | bytes 11534336 | tf_op jit(solution)/shard_map/scatter-add | solution.py:105
  1184.7 35.0 %collective-permute-done.13 = bf16[2048,256]{1,0:T(8,128)(2,1)S(1)} collective-permute-done((bf16[2048,256]{1,0:T(8,128)(2,1)S(1)}, bf16[2048,256]{1,0:T(8,128)(2,1)S(1)}, u32[]{:S(2)}, u32[]{:S(2)}) %collective-permute-start.13) | collective-permute-done | bytes 1048608 | tf_op jit(solution)/shard_map/ppermute | solution.py:23
  1220.4 10.5 fusion.25
  1277.3 142.9 %all-reduce.5.cloned.1.call-done = f32[1156352]{0:T(1024)} async-done(((f32[1156352]{0:T(1024)}), f32[1156352]{0:T(1024)}) %all-reduce.5.cloned.1.call-update) | async-done | bytes 4625424 | tf_op jit(solution)/shard_map/psum | solution.py:229
  (557 shorter events, 375.4 us)
Async XLA Ops:
  7.2 144.1 %all-reduce.7.cloned.1.call-start = ((), (), s32[]{:S(2)}) async-start(), calls=%async_computation.6 | async-start | bytes 4628480
  8.4 145.8 %copy-start.128 = (bf16[1,78,512]{2,1,0:T(8,128)(2,1)S(1)}, bf16[1,78,512]{2,1,0:T(8,128)(2,1)}, u32[]{:S(2)}) copy-start(bf16[1,78,512]{2,1,0:T(8,128)(2,1)} %param.39) | copy-start | bytes 239620
  12.3 146.2 %copy-start.156 = (s32[512,1]{0,1:T(1,128)}, s32[512,1]{0,1:T(1,128)S(1)}, u32[]{:S(2)}) copy-start(s32[512,1]{0,1:T(1,128)S(1)} %compare_select_fusion.6) | copy-start | bytes 6148
  15.6 15.6 %all-to-all-start = ((s32[16,1,64]{2,1,0:T(1,128)}), s32[16,1,64]{2,1,0:T(1,128)S(1)}, u32[]{:S(2)}, u32[]{:S(2)}) async-start(s32[16,1,64]{2,1,0:T(1,128)} %all_to_all.18), calls=%async_computation | async-start | bytes 16384 | tf_op jit(solution)/shard_map/all_to_all | solution.py:145
  32.4 145.1 %copy-start.162 = (s32[1024]{0:T(1024)}, s32[1024]{0:T(1024)S(1)}, u32[]{:S(2)}) copy-start(s32[1024]{0:T(1024)S(1)} %eq.50) | copy-start | bytes 12292
  158.5 19.1 %all-to-all-start.1 = ((bf16[16,64,256]{2,1,0:T(8,128)(2,1)}), bf16[16,64,256]{2,1,0:T(8,128)(2,1)}, u32[]{:S(2)}, u32[]{:S(2)}) async-start(bf16[16,64,256]{2,1,0:T(8,128)(2,1)} %bitcast.10), calls=%async_computation.1 | async-start | bytes 1048576 | tf_op jit(solution)/shard_map/all_to_all | solution.py:142
  184.5 42.5 %copy-start.34 = (bf16[2048,256]{1,0:T(8,128)(2,1)}, bf16[2048,256]{1,0:T(8,128)(2,1)S(1)}, u32[]{:S(2)}) copy-start(bf16[2048,256]{1,0:T(8,128)(2,1)S(1)} %convolution_convert_fusion.3) | copy-start | bytes 3145732
  184.5 42.5 %collective-permute-start = (bf16[2048,256]{1,0:T(8,128)(2,1)S(1)}, bf16[2048,256]{1,0:T(8,128)(2,1)S(1)}, u32[]{:S(2)}, u32[]{:S(2)}) collective-permute-start(bf16[2048,256]{1,0:T(8,128)(2,1)S(1)} %convolution_convert_fusion.3), channel_id=1, source_target_pairs={{0,1},{1,2},{2,3},{3,4},{4,5},{5,6},{6,7},{7,8},{8,9},{9,10},{10,1... | collective-permute-start | bytes 3145736 | tf_op jit(solution)/shard_map/ppermute | solution.py:23
  185.1 44.0 %collective-permute-start.1 = (bf16[2048,256]{1,0:T(8,128)(2,1)S(1)}, bf16[2048,256]{1,0:T(8,128)(2,1)}, u32[]{:S(2)}, u32[]{:S(2)}) collective-permute-start(bf16[2048,256]{1,0:T(8,128)(2,1)S(1)} %convolution_convert_fusion.3), channel_id=1, source_target_pairs={{1,0},{2,1},{3,2},{4,3},{5,4},{6,5},{7,6},{8,7},{9,8},{10,9},{11,1... | collective-permute-start | bytes 3145736 | tf_op jit(solution)/shard_map/ppermute | solution.py:24
  190.4 36.6 %copy-start.148 = (s32[2048,1]{0,1:T(1,128)}, s32[2048,1]{0,1:T(1,128)S(1)}, u32[]{:S(2)}) copy-start(s32[2048,1]{0,1:T(1,128)S(1)} %get-tuple-element.214) | copy-start | bytes 24580
  190.5 36.6 %copy-start.149 = (s32[2048,1]{0,1:T(1,128)}, s32[2048,1]{0,1:T(1,128)S(1)}, u32[]{:S(2)}) copy-start(s32[2048,1]{0,1:T(1,128)S(1)} %get-tuple-element.215) | copy-start | bytes 24580
  190.5 36.6 %copy-start.150 = (s32[2048,1]{0,1:T(1,128)}, s32[2048,1]{0,1:T(1,128)S(1)}, u32[]{:S(2)}) copy-start(s32[2048,1]{0,1:T(1,128)S(1)} %get-tuple-element.216) | copy-start | bytes 24580
  190.5 36.6 %copy-start.151 = (s32[2048,1]{0,1:T(1,128)}, s32[2048,1]{0,1:T(1,128)S(1)}, u32[]{:S(2)}) copy-start(s32[2048,1]{0,1:T(1,128)S(1)} %get-tuple-element.217) | copy-start | bytes 24580
  190.5 36.6 %copy-start.152 = (s32[2048,1]{0,1:T(1,128)}, s32[2048,1]{0,1:T(1,128)S(1)}, u32[]{:S(2)}) copy-start(s32[2048,1]{0,1:T(1,128)S(1)} %get-tuple-element.218) | copy-start | bytes 24580
  192.5 103.7 %copy-start.107 = (bf16[256,256]{1,0:T(8,128)(2,1)}, bf16[256,256]{1,0:T(8,128)(2,1)S(1)}, u32[]{:S(2)}) copy-start(bf16[256,256]{1,0:T(8,128)(2,1)S(1)} %slice.654) | copy-start | bytes 393220
  192.5 104.1 %copy-start.84 = (bf16[256,256]{1,0:T(8,128)(2,1)}, bf16[256,256]{1,0:T(8,128)(2,1)S(1)}, u32[]{:S(2)}) copy-start(bf16[256,256]{1,0:T(8,128)(2,1)S(1)} %slice.656) | copy-start | bytes 393220
  193.3 109.2 %copy-start.80 = (bf16[256,256]{1,0:T(8,128)(2,1)}, bf16[256,256]{1,0:T(8,128)(2,1)S(1)}, u32[]{:S(2)}) copy-start(bf16[256,256]{1,0:T(8,128)(2,1)S(1)} %slice.661) | copy-start | bytes 393220
  303.9 42.7 %copy-start.35 = (bf16[2048,256]{1,0:T(8,128)(2,1)}, bf16[2048,256]{1,0:T(8,128)(2,1)S(1)}, u32[]{:S(2)}) copy-start(bf16[2048,256]{1,0:T(8,128)(2,1)S(1)} %convolution_convert_fusion.2) | copy-start | bytes 3145732
  303.9 42.7 %collective-permute-start.2 = (bf16[2048,256]{1,0:T(8,128)(2,1)S(1)}, bf16[2048,256]{1,0:T(8,128)(2,1)S(1)}, u32[]{:S(2)}, u32[]{:S(2)}) collective-permute-start(bf16[2048,256]{1,0:T(8,128)(2,1)S(1)} %convolution_convert_fusion.2), channel_id=1, source_target_pairs={{0,1},{1,2},{2,3},{3,4},{4,5},{5,6},{6,7},{7,8},{8,9},{9,10},{10,1... | collective-permute-start | bytes 3145736 | tf_op jit(solution)/shard_map/ppermute | solution.py:23
  305.5 48.6 %collective-permute-start.3 = (bf16[2048,256]{1,0:T(8,128)(2,1)S(1)}, bf16[2048,256]{1,0:T(8,128)(2,1)}, u32[]{:S(2)}, u32[]{:S(2)}) collective-permute-start(bf16[2048,256]{1,0:T(8,128)(2,1)S(1)} %convolution_convert_fusion.2), channel_id=1, source_target_pairs={{1,0},{2,1},{3,2},{4,3},{5,4},{6,5},{7,6},{8,7},{9,8},{10,9},{11,1... | collective-permute-start | bytes 3145736 | tf_op jit(solution)/shard_map/ppermute | solution.py:24
  310.7 110.4 %copy-start.109 = (bf16[256,256]{1,0:T(8,128)(2,1)}, bf16[256,256]{1,0:T(8,128)(2,1)S(1)}, u32[]{:S(2)}) copy-start(bf16[256,256]{1,0:T(8,128)(2,1)S(1)} %slice.666) | copy-start | bytes 393220
  310.8 110.8 %copy-start.86 = (bf16[256,256]{1,0:T(8,128)(2,1)}, bf16[256,256]{1,0:T(8,128)(2,1)S(1)}, u32[]{:S(2)}) copy-start(bf16[256,256]{1,0:T(8,128)(2,1)S(1)} %slice.668) | copy-start | bytes 393220
  311.6 115.4 %copy-start.82 = (bf16[256,256]{1,0:T(8,128)(2,1)}, bf16[256,256]{1,0:T(8,128)(2,1)S(1)}, u32[]{:S(2)}) copy-start(bf16[256,256]{1,0:T(8,128)(2,1)S(1)} %slice.673) | copy-start | bytes 393220
  428.4 44.9 %copy-start.36 = (bf16[2048,256]{1,0:T(8,128)(2,1)}, bf16[2048,256]{1,0:T(8,128)(2,1)S(1)}, u32[]{:S(2)}) copy-start(bf16[2048,256]{1,0:T(8,128)(2,1)S(1)} %convolution_convert_fusion.1) | copy-start | bytes 3145732
  428.4 44.9 %collective-permute-start.4 = (bf16[2048,256]{1,0:T(8,128)(2,1)S(1)}, bf16[2048,256]{1,0:T(8,128)(2,1)S(1)}, u32[]{:S(2)}, u32[]{:S(2)}) collective-permute-start(bf16[2048,256]{1,0:T(8,128)(2,1)S(1)} %convolution_convert_fusion.1), channel_id=1, source_target_pairs={{0,1},{1,2},{2,3},{3,4},{4,5},{5,6},{6,7},{7,8},{8,9},{9,10},{10,1... | collective-permute-start | bytes 3145736 | tf_op jit(solution)/shard_map/ppermute | solution.py:23
  428.8 46.6 %collective-permute-start.5 = (bf16[2048,256]{1,0:T(8,128)(2,1)S(1)}, bf16[2048,256]{1,0:T(8,128)(2,1)}, u32[]{:S(2)}, u32[]{:S(2)}) collective-permute-start(bf16[2048,256]{1,0:T(8,128)(2,1)S(1)} %convolution_convert_fusion.1), channel_id=1, source_target_pairs={{1,0},{2,1},{3,2},{4,3},{5,4},{6,5},{7,6},{8,7},{9,8},{10,9},{11,1... | collective-permute-start | bytes 3145736 | tf_op jit(solution)/shard_map/ppermute | solution.py:24
  434.3 98.9 %copy-start.125 = (bf16[256,256]{1,0:T(8,128)(2,1)}, bf16[256,256]{1,0:T(8,128)(2,1)S(1)}, u32[]{:S(2)}) copy-start(bf16[256,256]{1,0:T(8,128)(2,1)S(1)} %slice.675) | copy-start | bytes 393220
  434.4 105.4 %copy-start.111 = (bf16[256,256]{1,0:T(8,128)(2,1)}, bf16[256,256]{1,0:T(8,128)(2,1)S(1)}, u32[]{:S(2)}) copy-start(bf16[256,256]{1,0:T(8,128)(2,1)S(1)} %slice.678) | copy-start | bytes 393220
  434.4 105.7 %copy-start.88 = (bf16[256,256]{1,0:T(8,128)(2,1)}, bf16[256,256]{1,0:T(8,128)(2,1)S(1)}, u32[]{:S(2)}) copy-start(bf16[256,256]{1,0:T(8,128)(2,1)S(1)} %slice.680) | copy-start | bytes 393220
  546.7 20.7 %all-to-all-start.2 = ((bf16[16,64,256]{2,1,0:T(8,128)(2,1)}), bf16[16,64,256]{2,1,0:T(8,128)(2,1)}, u32[]{:S(2)}, u32[]{:S(2)}) async-start(bf16[16,64,256]{2,1,0:T(8,128)(2,1)} %bitcast.293), calls=%async_computation.2 | async-start | bytes 1048576 | tf_op jit(solution)/shard_map/all_to_all | solution.py:163
  552.8 6.5 collective-permute-start.6
  574.6 9.3 collective-permute-start.7
  655.2 6.4 collective-permute-start.8
  670.4 18.6 %all-to-all-start.3 = ((bf16[16,64,256]{2,1,0:T(8,128)(2,1)}), bf16[16,64,256]{2,1,0:T(8,128)(2,1)}, u32[]{:S(2)}, u32[]{:S(2)}) async-start(bf16[16,64,256]{2,1,0:T(8,128)(2,1)} %bitcast.287), calls=%async_computation.3 | async-start | bytes 1048576 | tf_op jit(solution)/shard_map/all_to_all | solution.py:194
  814.4 26.4 %collective-permute-start.10 = (bf16[2048,256]{1,0:T(8,128)(2,1)}, bf16[2048,256]{1,0:T(8,128)(2,1)}, u32[]{:S(2)}, u32[]{:S(2)}) collective-permute-start(bf16[2048,256]{1,0:T(8,128)(2,1)} %get-tuple-element.185), channel_id=1, source_target_pairs={{1,0},{2,1},{3,2},{4,3},{5,4},{6,5},{7,6},{8,7},{9,8},{10,9},{11,1... | collective-permute-start | bytes 3145736 | tf_op jit(solution)/shard_map/ppermute | solution.py:24
  816.9 39.7 %collective-permute-start.9 = (bf16[2048,256]{1,0:T(8,128)(2,1)S(1)}, bf16[2048,256]{1,0:T(8,128)(2,1)}, u32[]{:S(2)}, u32[]{:S(2)}) collective-permute-start(bf16[2048,256]{1,0:T(8,128)(2,1)S(1)} %get-tuple-element.184), channel_id=1, source_target_pairs={{0,1},{1,2},{2,3},{3,4},{4,5},{5,6},{6,7},{7,8},{8,9},{9,10},{10,1... | collective-permute-start | bytes 3145736 | tf_op jit(solution)/shard_map/ppermute | solution.py:23
  988.6 47.7 %collective-permute-start.11 = (bf16[2048,256]{1,0:T(8,128)(2,1)S(1)}, bf16[2048,256]{1,0:T(8,128)(2,1)S(1)}, u32[]{:S(2)}, u32[]{:S(2)}) collective-permute-start(bf16[2048,256]{1,0:T(8,128)(2,1)S(1)} %get-tuple-element.182), channel_id=1, source_target_pairs={{0,1},{1,2},{2,3},{3,4},{4,5},{5,6},{6,7},{7,8},{8,9},{9,10},{10,1... | collective-permute-start | bytes 3145736 | tf_op jit(solution)/shard_map/ppermute | solution.py:23
  991.2 45.8 %collective-permute-start.12 = (bf16[2048,256]{1,0:T(8,128)(2,1)S(1)}, bf16[2048,256]{1,0:T(8,128)(2,1)S(1)}, u32[]{:S(2)}, u32[]{:S(2)}) collective-permute-start(bf16[2048,256]{1,0:T(8,128)(2,1)S(1)} %get-tuple-element.183), channel_id=1, source_target_pairs={{1,0},{2,1},{3,2},{4,3},{5,4},{6,5},{7,6},{8,7},{9,8},{10,9},{11,1... | collective-permute-start | bytes 3145736 | tf_op jit(solution)/shard_map/ppermute | solution.py:24
  1000.3 47.5 %copy-start.78 = (f32[5,256,256]{2,1,0:T(8,128)}, f32[5,256,256]{2,1,0:T(8,128)S(1)}, u32[]{:S(2)}) copy-start(f32[5,256,256]{2,1,0:T(8,128)S(1)} %fusion.35) | copy-start | bytes 3932164
  1000.3 47.5 %copy-start.7 = (bf16[2048,256]{1,0:T(8,128)(2,1)S(1)}, bf16[2048,256]{1,0:T(8,128)(2,1)}, u32[]{:S(2)}) copy-start(bf16[2048,256]{1,0:T(8,128)(2,1)} %copy-done.5) | copy-start | bytes 3145732
  1173.5 46.2 %collective-permute-start.13 = (bf16[2048,256]{1,0:T(8,128)(2,1)S(1)}, bf16[2048,256]{1,0:T(8,128)(2,1)S(1)}, u32[]{:S(2)}, u32[]{:S(2)}) collective-permute-start(bf16[2048,256]{1,0:T(8,128)(2,1)S(1)} %get-tuple-element.180), channel_id=1, source_target_pairs={{0,1},{1,2},{2,3},{3,4},{4,5},{5,6},{6,7},{7,8},{8,9},{9,10},{10,1... | collective-permute-start | bytes 3145736 | tf_op jit(solution)/shard_map/ppermute | solution.py:23
  1175.3 45.2 %collective-permute-start.14 = (bf16[2048,256]{1,0:T(8,128)(2,1)S(1)}, bf16[2048,256]{1,0:T(8,128)(2,1)S(1)}, u32[]{:S(2)}, u32[]{:S(2)}) collective-permute-start(bf16[2048,256]{1,0:T(8,128)(2,1)S(1)} %get-tuple-element.181), channel_id=1, source_target_pairs={{1,0},{2,1},{3,2},{4,3},{5,4},{6,5},{7,6},{8,7},{9,8},{10,9},{11,1... | collective-permute-start | bytes 3145736 | tf_op jit(solution)/shard_map/ppermute | solution.py:24
  1184.7 46.3 %copy-start.4 = (bf16[2048,256]{1,0:T(8,128)(2,1)S(1)}, bf16[2048,256]{1,0:T(8,128)(2,1)}, u32[]{:S(2)}) copy-start(bf16[2048,256]{1,0:T(8,128)(2,1)} %copy-done.2) | copy-start | bytes 3145732
  1239.6 20.9 %all-to-all-start.4 = ((bf16[16,64,256]{2,1,0:T(8,128)(2,1)}), bf16[16,64,256]{2,1,0:T(8,128)(2,1)S(1)}, u32[]{:S(2)}, u32[]{:S(2)}) async-start(bf16[16,64,256]{2,1,0:T(8,128)(2,1)} %bitcast.28), calls=%async_computation.4 | async-start | bytes 1048576 | tf_op jit(solution)/shard_map/all_to_all | solution.py:211
  1245.5 174.6 %all-reduce.5.cloned.1.call-start = ((), (), s32[]{:S(2)}) async-start(), calls=%async_computation.5 | async-start | bytes 9256960 | tf_op jit(solution)/shard_map/psum | solution.py:229
  1277.3 147.2 %copy-start.103 = (f32[36136]{0:T(1024)S(1)}, f32[36136]{0:T(1024)}, u32[]{:S(2)}) copy-start(f32[36136]{0:T(1024)} %param.36) | copy-start | bytes 433636
  1277.3 147.2 %copy-start.134 = (f32[36136]{0:T(1024)S(1)}, f32[36136]{0:T(1024)}, u32[]{:S(2)}) copy-start(f32[36136]{0:T(1024)} %param.37) | copy-start | bytes 433636
  1277.3 147.2 %copy-start.135 = (f32[36136]{0:T(1024)S(1)}, f32[36136]{0:T(1024)}, u32[]{:S(2)}) copy-start(f32[36136]{0:T(1024)} %param.38) | copy-start | bytes 433636
  (148 other events, 746.1 us)
Sparse Core Ops, SparseCore 0:
  13.6 137.6 all-reduce.6
  1276.6 143.5 all-reduce.4
where the time goes:
time: 1450 us; the launch traced here: 1430 us
  waiting for transfers between devices  526 us (36%)
  other arithmetic  393 us (27%)
  local copies, waits for them, and re-layouts  277 us (19%)
  matrix products  102 us (7%)
  starting transfers between devices  70.3 us (5%)
  blocking collectives  47.1 us (3%)
  between operations  19.7 us (1%)
    scatter-add x18, other arithmetic, round_backward(): grad_pad = grad_pad.at[places[:, edge]].add(grad_edge)  320 us
    ppermute x6, waiting for transfers between devices, extended(): before = lax.ppermute(last, axis, up)  194 us
    gather x18, local copies, waits for them, and re-layouts, edge_inputs(): return padded[places[:, edge]].astype(jnp.float32) + dest  169 us
    psum x1, waiting for transfers between devices, shards(): summed = lax.psum(flat, ('dp', 'space'))  143 us
    unnamed x3, waiting for transfers between devices  119 us
    dot_general x59, matrix products, inner(): lax.dot_general(left, right, (((left_dim,), (right_dim,)), ((), ())), pre...  102 us
    unnamed x362, local copies, waits for them, and re-layouts  58.1 us
    psum x1, blocking collectives, shards(): total, count = lax.psum((local_total, jnp.sum(counted)), ('dp', 'space'))  47.1 us
  transfers between devices with their start and end apart: 22, of which 21 were waited for; matrix products, arithmetic and copies ran while one was open for 4% of the time, Pallas kernels for 0%

commit v1 on v0

--- a/solution.py
+++ b/solution.py
@@ -226,7 +226,7 @@
     ]
     flat = jnp.concatenate([piece.reshape(-1) for piece in pieces])
     flat = jnp.concatenate([flat, jnp.zeros((everything.shape[0] - flat.shape[0],), jnp.float32)])
-    summed = lax.psum(flat, ("dp", "space"))
+    summed = jnp.sum(lax.all_gather(flat, ("dp", "space")), axis=0)
     norm = jnp.sqrt(jnp.sum(summed * summed))
     mine = lax.dynamic_slice_in_dim(summed, lax.axis_index(("dp", "space")) * shard, shard)
     clipped = mine * jnp.minimum(1.0, 0.05 / norm)

time: 1450 us -> 2200 us (1.52)
  waiting for transfers between devices: 526 us -> 1130 us
  other arithmetic: 393 us -> 520 us
    all_gather x0 -> x1, waiting for transfers between devices: none -> 742 us  [shards(): summed = jnp.sum(lax.all_gather(flat, ('dp', 'space')), axis=0)]
    psum x1 -> x0, waiting for transfers between devices: 143 us -> none  [shards(): summed = lax.psum(flat, ('dp', 'space'))]
    reduce_sum x0 -> x1, other arithmetic: none -> 125 us  [shards(): summed = jnp.sum(lax.all_gather(flat, ('dp', 'space')), axis=0)]
    ppermute x6, waiting for transfers between devices: 28.8 us -> 73.9 us  [extended(): after = lax.ppermute(initial, axis, down)]
    ppermute x6, waiting for transfers between devices: 194 us -> 149 us  [extended(): before = lax.ppermute(last, axis, up)]
    unnamed x362 -> x339, local copies, waits for them, and re-layouts: 58.1 us -> 74.1 us
  transfers between devices with their start and end apart: 22 -> 22, of which waited for: 21 -> 21; matrix products, arithmetic and copies ran while one was open for 4% -> 2% of each run, Pallas kernels for 0% -> 0%
where the time goes in v1:
time: 2200 us; the launch traced here: 2190 us
  waiting for transfers between devices  1130 us (51%)
  other arithmetic  520 us (24%)
  local copies, waits for them, and re-layouts  294 us (13%)
  matrix products  109 us (5%)
  starting transfers between devices  71.4 us (3%)
  blocking collectives  47 us (2%)
    all_gather x1, waiting for transfers between devices, shards(): summed = jnp.sum(lax.all_gather(flat, ('dp', 'space')), axis=0)  742 us
    scatter-add x18, other arithmetic, round_backward(): grad_pad = grad_pad.at[places[:, edge]].add(grad_edge)  321 us
    gather x18, local copies, waits for them, and re-layouts, edge_inputs(): return padded[places[:, edge]].astype(jnp.float32) + dest  171 us
    ppermute x6, waiting for transfers between devices, extended(): before = lax.ppermute(last, axis, up)  149 us
    reduce_sum x1, other arithmetic, shards(): summed = jnp.sum(lax.all_gather(flat, ('dp', 'space')), axis=0)  125 us
    unnamed x3, waiting for transfers between devices  119 us
    dot_general x59, matrix products, inner(): lax.dot_general(left, right, (((left_dim,), (right_dim,)), ((), ())), pre...  109 us
    unnamed x339, local copies, waits for them, and re-layouts  74.1 us
  transfers between devices with their start and end apart: 22, of which 21 were waited for; matrix products, arithmetic and copies ran while one was open for 2% of the time, Pallas kernels for 0%

profile of v1, /device:TPU:0, one launch (start us, length us, event | category | flops | bytes accessed | tf_op | source)
XLA Modules:
  0.0 2188.6 jit_solution(12063834149118174033)
XLA Ops:
  32.4 118.8 %all-reduce.4.cloned.1.call-done = bf16[1156352]{0:T(1024)(128)(2,1)} async-done(((bf16[1156352]{0:T(1024)(128)(2,1)}), bf16[1156352]{0:T(1024)(128)(2,1)}) %all-reduce.4.cloned.1.call-update) | async-done | bytes 2312720
  164.6 12.9 all-to-all-done.1
  190.8 19.9 collective-permute-done.1
  211.7 16.5 collective-permute-done
  230.4 9.7 gather_fusion.5
  240.1 9.7 gather_fusion.4
  249.8 9.7 gather_fusion.3
  268.5 9.7 gather_fusion.1
  310.1 19.5 collective-permute-done.3
  330.6 18.7 collective-permute-done.2
  351.4 9.7 gather_fusion.11
  361.1 9.7 gather_fusion.10
  370.8 9.7 gather_fusion.9
  389.5 9.7 gather_fusion.7
  431.0 19.9 collective-permute-done.5
  452.0 21.6 collective-permute-done.4
  475.8 9.7 gather_fusion.17
  485.5 9.8 gather_fusion.16
  495.2 9.7 gather_fusion.15
  513.9 9.7 gather_fusion.13
  593.4 47.0 %all-reduce.1 = (f32[1]{0:T(128)}, f32[]{:T(128)}) all-reduce(f32[1]{0:T(128)} %bitcast.23, f32[]{:T(128)} %fusion.67), channel_id=1, replica_groups=mesh['dp'=2,'space'=16] {'dp','space'}, use_global_device_ids=true, to_apply=%region_7.8 | all-reduce | flops 2 | bytes 16 | tf_op jit(solution)/shard_map/psum | solution.py:181
  676.1 12.4 all-to-all-done.3
  702.9 15.8 scatter_custom_fusion.4
  718.7 18.3 scatter_custom_fusion.5
  737.0 18.2 scatter_custom_fusion.6
  755.2 18.2 scatter_custom_fusion.7
  773.4 18.2 scatter_custom_fusion.8
  791.6 18.2 scatter_custom_fusion.9
  825.1 29.6 %collective-permute-done.9 = bf16[2048,256]{1,0:T(8,128)(2,1)} collective-permute-done((bf16[2048,256]{1,0:T(8,128)(2,1)S(1)}, bf16[2048,256]{1,0:T(8,128)(2,1)}, u32[]{:S(2)}, u32[]{:S(2)}) %collective-permute-start.9) | collective-permute-done | bytes 1048608 | tf_op jit(solution)/shard_map/ppermute | solution.py:23
  880.0 16.0 scatter_custom_fusion.10
  896.0 18.2 scatter_custom_fusion.11
  914.2 18.2 scatter_custom_fusion.12
  932.4 18.2 scatter_custom_fusion.13
  950.5 18.2 scatter_custom_fusion.14
  968.7 18.2 scatter_custom_fusion.15
  1001.1 29.5 %collective-permute-done.11 = bf16[2048,256]{1,0:T(8,128)(2,1)S(1)} collective-permute-done((bf16[2048,256]{1,0:T(8,128)(2,1)S(1)}, bf16[2048,256]{1,0:T(8,128)(2,1)S(1)}, u32[]{:S(2)}, u32[]{:S(2)}) %collective-permute-start.11) | collective-permute-done | bytes 1048608 | tf_op jit(solution)/shard_map/ppermute | solution.py:23
  1039.9 10.4 fusion.27
  1067.8 16.0 scatter_custom_fusion.16
  1083.7 18.2 scatter_custom_fusion.17
  1101.9 18.2 scatter_custom_fusion.18
  1120.1 18.2 scatter_custom_fusion.19
  1138.3 18.4 scatter_custom_fusion.20
  1156.6 18.2 scatter_custom_fusion.21
  1188.6 33.2 %collective-permute-done.13 = bf16[2048,256]{1,0:T(8,128)(2,1)S(1)} collective-permute-done((bf16[2048,256]{1,0:T(8,128)(2,1)S(1)}, bf16[2048,256]{1,0:T(8,128)(2,1)S(1)}, u32[]{:S(2)}, u32[]{:S(2)}) %collective-permute-start.13) | collective-permute-done | bytes 1048608 | tf_op jit(solution)/shard_map/ppermute | solution.py:23
  1225.1 11.0 fusion.25
  1287.0 18.9 reshape.940
  1306.7 742.2 %all-gather.4.cloned.1.call-done = f32[32,1,1156352]{2,1,0:T(1,128)} async-done(((f32[1,1,1156352]{2,1,0:T(1,128)}), f32[32,1,1156352]{2,1,0:T(1,128)}) %all-gather.4.cloned.1.call-update) | async-done | bytes 148013072 | tf_op jit(solution)/shard_map/all_gather | solution.py:229
  2048.9 125.3 %reduce_sum.148 = f32[1156352]{0:T(1024)} reduce(f32[32,1,1156352]{2,1,0:T(1,128)} %all-gather.4.cloned.1.call-done, f32[]{:T(128)} %constant.352.clone.1), dimensions={0,1}, to_apply=%region_40.41 | reduce | flops 35846912 | bytes 152638464 | tf_op jit(solution)/shard_map/reduce_sum | solution.py:229
  (535 shorter events, 424.5 us)
Async XLA Ops:
  7.2 144.1 %all-reduce.4.cloned.1.call-start = ((), (), s32[]{:S(2)}) async-start(), calls=%async_computation.5 | async-start | bytes 4628480
  8.4 145.8 %copy-start.118 = (bf16[1,78,512]{2,1,0:T(8,128)(2,1)S(1)}, bf16[1,78,512]{2,1,0:T(8,128)(2,1)}, u32[]{:S(2)}) copy-start(bf16[1,78,512]{2,1,0:T(8,128)(2,1)} %param.39) | copy-start | bytes 239620
  12.3 146.3 %copy-start.144 = (s32[512,1]{0,1:T(1,128)}, s32[512,1]{0,1:T(1,128)S(1)}, u32[]{:S(2)}) copy-start(s32[512,1]{0,1:T(1,128)S(1)} %compare_select_fusion.6) | copy-start | bytes 6148
  15.6 15.6 all-to-all-start
  32.4 145.1 %copy-start.150 = (s32[1024]{0:T(1024)}, s32[1024]{0:T(1024)S(1)}, u32[]{:S(2)}) copy-start(s32[1024]{0:T(1024)S(1)} %eq.50) | copy-start | bytes 12292
  158.5 19.0 all-to-all-start.1
  184.5 26.2 %copy-start.33 = (bf16[2048,256]{1,0:T(8,128)(2,1)}, bf16[2048,256]{1,0:T(8,128)(2,1)S(1)}, u32[]{:S(2)}) copy-start(bf16[2048,256]{1,0:T(8,128)(2,1)S(1)} %convolution_convert_fusion.3) | copy-start | bytes 3145732
  184.5 26.2 %collective-permute-start.1 = (bf16[2048,256]{1,0:T(8,128)(2,1)S(1)}, bf16[2048,256]{1,0:T(8,128)(2,1)S(1)}, u32[]{:S(2)}, u32[]{:S(2)}) collective-permute-start(bf16[2048,256]{1,0:T(8,128)(2,1)S(1)} %convolution_convert_fusion.3), channel_id=1, source_target_pairs={{1,0},{2,1},{3,2},{4,3},{5,4},{6,5},{7,6},{8,7},{9,8},{10,9},{11,1... | collective-permute-start | bytes 3145736 | tf_op jit(solution)/shard_map/ppermute | solution.py:24
  187.0 41.2 %collective-permute-start = (bf16[2048,256]{1,0:T(8,128)(2,1)S(1)}, bf16[2048,256]{1,0:T(8,128)(2,1)}, u32[]{:S(2)}, u32[]{:S(2)}) collective-permute-start(bf16[2048,256]{1,0:T(8,128)(2,1)S(1)} %convolution_convert_fusion.3), channel_id=1, source_target_pairs={{0,1},{1,2},{2,3},{3,4},{4,5},{5,6},{6,7},{7,8},{8,9},{9,10},{10,1... | collective-permute-start | bytes 3145736 | tf_op jit(solution)/shard_map/ppermute | solution.py:23
  187.4 23.3 %copy-start.136 = (s32[2048,1]{0,1:T(1,128)}, s32[2048,1]{0,1:T(1,128)S(1)}, u32[]{:S(2)}) copy-start(s32[2048,1]{0,1:T(1,128)S(1)} %get-tuple-element.224) | copy-start | bytes 24580
  187.4 23.3 %copy-start.137 = (s32[2048,1]{0,1:T(1,128)}, s32[2048,1]{0,1:T(1,128)S(1)}, u32[]{:S(2)}) copy-start(s32[2048,1]{0,1:T(1,128)S(1)} %get-tuple-element.225) | copy-start | bytes 24580
  187.4 23.3 %copy-start.138 = (s32[2048,1]{0,1:T(1,128)}, s32[2048,1]{0,1:T(1,128)S(1)}, u32[]{:S(2)}) copy-start(s32[2048,1]{0,1:T(1,128)S(1)} %get-tuple-element.226) | copy-start | bytes 24580
  187.4 23.3 %copy-start.139 = (s32[2048,1]{0,1:T(1,128)}, s32[2048,1]{0,1:T(1,128)S(1)}, u32[]{:S(2)}) copy-start(s32[2048,1]{0,1:T(1,128)S(1)} %get-tuple-element.227) | copy-start | bytes 24580
  187.4 23.3 %copy-start.140 = (s32[2048,1]{0,1:T(1,128)}, s32[2048,1]{0,1:T(1,128)S(1)}, u32[]{:S(2)}) copy-start(s32[2048,1]{0,1:T(1,128)S(1)} %get-tuple-element.228) | copy-start | bytes 24580
  187.4 23.3 %copy-start.141 = (s32[2048,1]{0,1:T(1,128)}, s32[2048,1]{0,1:T(1,128)S(1)}, u32[]{:S(2)}) copy-start(s32[2048,1]{0,1:T(1,128)S(1)} %get-tuple-element.229) | copy-start | bytes 24580
  189.3 112.3 %copy-start.72 = (bf16[256,256]{1,0:T(8,128)(2,1)}, bf16[256,256]{1,0:T(8,128)(2,1)S(1)}, u32[]{:S(2)}) copy-start(bf16[256,256]{1,0:T(8,128)(2,1)S(1)} %slice.661) | copy-start | bytes 393220
  190.1 105.7 %copy-start.76 = (bf16[256,256]{1,0:T(8,128)(2,1)}, bf16[256,256]{1,0:T(8,128)(2,1)S(1)}, u32[]{:S(2)}) copy-start(bf16[256,256]{1,0:T(8,128)(2,1)S(1)} %slice.656) | copy-start | bytes 393220
  190.1 105.2 %copy-start.97 = (bf16[256,256]{1,0:T(8,128)(2,1)}, bf16[256,256]{1,0:T(8,128)(2,1)S(1)}, u32[]{:S(2)}) copy-start(bf16[256,256]{1,0:T(8,128)(2,1)S(1)} %slice.654) | copy-start | bytes 393220
  303.0 26.6 %copy-start.34 = (bf16[2048,256]{1,0:T(8,128)(2,1)}, bf16[2048,256]{1,0:T(8,128)(2,1)S(1)}, u32[]{:S(2)}) copy-start(bf16[2048,256]{1,0:T(8,128)(2,1)S(1)} %convolution_convert_fusion.2) | copy-start | bytes 3145732
  303.0 26.6 %collective-permute-start.3 = (bf16[2048,256]{1,0:T(8,128)(2,1)S(1)}, bf16[2048,256]{1,0:T(8,128)(2,1)S(1)}, u32[]{:S(2)}, u32[]{:S(2)}) collective-permute-start(bf16[2048,256]{1,0:T(8,128)(2,1)S(1)} %convolution_convert_fusion.2), channel_id=1, source_target_pairs={{1,0},{2,1},{3,2},{4,3},{5,4},{6,5},{7,6},{8,7},{9,8},{10,9},{11,1... | collective-permute-start | bytes 3145736 | tf_op jit(solution)/shard_map/ppermute | solution.py:24
  308.0 41.3 %collective-permute-start.2 = (bf16[2048,256]{1,0:T(8,128)(2,1)S(1)}, bf16[2048,256]{1,0:T(8,128)(2,1)}, u32[]{:S(2)}, u32[]{:S(2)}) collective-permute-start(bf16[2048,256]{1,0:T(8,128)(2,1)S(1)} %convolution_convert_fusion.2), channel_id=1, source_target_pairs={{0,1},{1,2},{2,3},{3,4},{4,5},{5,6},{6,7},{7,8},{8,9},{9,10},{10,1... | collective-permute-start | bytes 3145736 | tf_op jit(solution)/shard_map/ppermute | solution.py:23
  308.6 113.7 %copy-start.74 = (bf16[256,256]{1,0:T(8,128)(2,1)}, bf16[256,256]{1,0:T(8,128)(2,1)S(1)}, u32[]{:S(2)}) copy-start(bf16[256,256]{1,0:T(8,128)(2,1)S(1)} %slice.673) | copy-start | bytes 393220
  309.3 107.4 %copy-start.78 = (bf16[256,256]{1,0:T(8,128)(2,1)}, bf16[256,256]{1,0:T(8,128)(2,1)S(1)}, u32[]{:S(2)}) copy-start(bf16[256,256]{1,0:T(8,128)(2,1)S(1)} %slice.668) | copy-start | bytes 393220
  309.4 106.9 %copy-start.99 = (bf16[256,256]{1,0:T(8,128)(2,1)}, bf16[256,256]{1,0:T(8,128)(2,1)S(1)}, u32[]{:S(2)}) copy-start(bf16[256,256]{1,0:T(8,128)(2,1)S(1)} %slice.666) | copy-start | bytes 393220
  423.6 27.4 %copy-start.35 = (bf16[2048,256]{1,0:T(8,128)(2,1)}, bf16[2048,256]{1,0:T(8,128)(2,1)S(1)}, u32[]{:S(2)}) copy-start(bf16[2048,256]{1,0:T(8,128)(2,1)S(1)} %convolution_convert_fusion.1) | copy-start | bytes 3145732
  423.6 27.4 %collective-permute-start.5 = (bf16[2048,256]{1,0:T(8,128)(2,1)S(1)}, bf16[2048,256]{1,0:T(8,128)(2,1)S(1)}, u32[]{:S(2)}, u32[]{:S(2)}) collective-permute-start(bf16[2048,256]{1,0:T(8,128)(2,1)S(1)} %convolution_convert_fusion.1), channel_id=1, source_target_pairs={{1,0},{2,1},{3,2},{4,3},{5,4},{6,5},{7,6},{8,7},{9,8},{10,9},{11,1... | collective-permute-start | bytes 3145736 | tf_op jit(solution)/shard_map/ppermute | solution.py:24
  429.9 43.7 %collective-permute-start.4 = (bf16[2048,256]{1,0:T(8,128)(2,1)S(1)}, bf16[2048,256]{1,0:T(8,128)(2,1)}, u32[]{:S(2)}, u32[]{:S(2)}) collective-permute-start(bf16[2048,256]{1,0:T(8,128)(2,1)S(1)} %convolution_convert_fusion.1), channel_id=1, source_target_pairs={{0,1},{1,2},{2,3},{3,4},{4,5},{5,6},{6,7},{7,8},{8,9},{9,10},{10,1... | collective-permute-start | bytes 3145736 | tf_op jit(solution)/shard_map/ppermute | solution.py:23
  430.9 108.7 %copy-start.80 = (bf16[256,256]{1,0:T(8,128)(2,1)}, bf16[256,256]{1,0:T(8,128)(2,1)S(1)}, u32[]{:S(2)}) copy-start(bf16[256,256]{1,0:T(8,128)(2,1)S(1)} %slice.680) | copy-start | bytes 393220
  431.0 108.2 %copy-start.101 = (bf16[256,256]{1,0:T(8,128)(2,1)}, bf16[256,256]{1,0:T(8,128)(2,1)S(1)}, u32[]{:S(2)}) copy-start(bf16[256,256]{1,0:T(8,128)(2,1)S(1)} %slice.678) | copy-start | bytes 393220
  431.0 101.6 %copy-start.115 = (bf16[256,256]{1,0:T(8,128)(2,1)}, bf16[256,256]{1,0:T(8,128)(2,1)S(1)}, u32[]{:S(2)}) copy-start(bf16[256,256]{1,0:T(8,128)(2,1)S(1)} %slice.675) | copy-start | bytes 393220
  546.1 20.8 all-to-all-start.2
  552.4 20.2 copy-start.92
  553.1 7.0 collective-permute-start.6
  574.1 9.3 collective-permute-start.7
  640.4 23.2 %copy-start.122 = (bf16[256,78]{1,0:T(8,128)(2,1)S(1)}, bf16[256,78]{1,0:T(8,128)(2,1)}, u32[]{:S(2)}) copy-start(bf16[256,78]{1,0:T(8,128)(2,1)} %reshape.563) | copy-start | bytes 119812
  654.7 6.4 collective-permute-start.8
  663.6 25.0 %copy-start.152 = (s32[1024]{0:T(1024)S(1)}, s32[1024]{0:T(1024)}, u32[]{:S(2)}) copy-start(s32[1024]{0:T(1024)} %copy-done.150) | copy-start | bytes 12292
  669.9 18.6 all-to-all-start.3
  814.0 40.7 %collective-permute-start.9 = (bf16[2048,256]{1,0:T(8,128)(2,1)S(1)}, bf16[2048,256]{1,0:T(8,128)(2,1)}, u32[]{:S(2)}, u32[]{:S(2)}) collective-permute-start(bf16[2048,256]{1,0:T(8,128)(2,1)S(1)} %get-tuple-element.194), channel_id=1, source_target_pairs={{0,1},{1,2},{2,3},{3,4},{4,5},{5,6},{6,7},{7,8},{8,9},{9,10},{10,1... | collective-permute-start | bytes 3145736 | tf_op jit(solution)/shard_map/ppermute | solution.py:23
  814.6 42.1 %collective-permute-start.10 = (bf16[2048,256]{1,0:T(8,128)(2,1)}, bf16[2048,256]{1,0:T(8,128)(2,1)}, u32[]{:S(2)}, u32[]{:S(2)}) collective-permute-start(bf16[2048,256]{1,0:T(8,128)(2,1)} %get-tuple-element.195), channel_id=1, source_target_pairs={{1,0},{2,1},{3,2},{4,3},{5,4},{6,5},{7,6},{8,7},{9,8},{10,9},{11,1... | collective-permute-start | bytes 3145736 | tf_op jit(solution)/shard_map/ppermute | solution.py:24
  990.2 40.5 %collective-permute-start.11 = (bf16[2048,256]{1,0:T(8,128)(2,1)S(1)}, bf16[2048,256]{1,0:T(8,128)(2,1)S(1)}, u32[]{:S(2)}, u32[]{:S(2)}) collective-permute-start(bf16[2048,256]{1,0:T(8,128)(2,1)S(1)} %get-tuple-element.192), channel_id=1, source_target_pairs={{0,1},{1,2},{2,3},{3,4},{4,5},{5,6},{6,7},{7,8},{8,9},{9,10},{10,1... | collective-permute-start | bytes 3145736 | tf_op jit(solution)/shard_map/ppermute | solution.py:23
  990.8 49.1 %collective-permute-start.12 = (bf16[2048,256]{1,0:T(8,128)(2,1)S(1)}, bf16[2048,256]{1,0:T(8,128)(2,1)S(1)}, u32[]{:S(2)}, u32[]{:S(2)}) collective-permute-start(bf16[2048,256]{1,0:T(8,128)(2,1)S(1)} %get-tuple-element.193), channel_id=1, source_target_pairs={{1,0},{2,1},{3,2},{4,3},{5,4},{6,5},{7,6},{8,7},{9,8},{10,9},{11,1... | collective-permute-start | bytes 3145736 | tf_op jit(solution)/shard_map/ppermute | solution.py:24
  1001.1 49.2 %copy-start.7 = (bf16[2048,256]{1,0:T(8,128)(2,1)S(1)}, bf16[2048,256]{1,0:T(8,128)(2,1)}, u32[]{:S(2)}) copy-start(bf16[2048,256]{1,0:T(8,128)(2,1)} %copy-done.5) | copy-start | bytes 3145732
  1178.1 43.8 %collective-permute-start.13 = (bf16[2048,256]{1,0:T(8,128)(2,1)S(1)}, bf16[2048,256]{1,0:T(8,128)(2,1)S(1)}, u32[]{:S(2)}, u32[]{:S(2)}) collective-permute-start(bf16[2048,256]{1,0:T(8,128)(2,1)S(1)} %get-tuple-element.190), channel_id=1, source_target_pairs={{0,1},{1,2},{2,3},{3,4},{4,5},{5,6},{6,7},{7,8},{8,9},{9,10},{10,1... | collective-permute-start | bytes 3145736 | tf_op jit(solution)/shard_map/ppermute | solution.py:23
  1178.4 46.7 %collective-permute-start.14 = (bf16[2048,256]{1,0:T(8,128)(2,1)S(1)}, bf16[2048,256]{1,0:T(8,128)(2,1)S(1)}, u32[]{:S(2)}, u32[]{:S(2)}) collective-permute-start(bf16[2048,256]{1,0:T(8,128)(2,1)S(1)} %get-tuple-element.191), channel_id=1, source_target_pairs={{1,0},{2,1},{3,2},{4,3},{5,4},{6,5},{7,6},{8,7},{9,8},{10,9},{11,1... | collective-permute-start | bytes 3145736 | tf_op jit(solution)/shard_map/ppermute | solution.py:24
  1188.6 47.5 %copy-start.4 = (bf16[2048,256]{1,0:T(8,128)(2,1)S(1)}, bf16[2048,256]{1,0:T(8,128)(2,1)}, u32[]{:S(2)}) copy-start(bf16[2048,256]{1,0:T(8,128)(2,1)} %copy-done.2) | copy-start | bytes 3145732
  1249.6 21.4 all-to-all-start.4
  1255.8 793.1 %all-gather.4.cloned.1.call-start = ((), (), s32[]{:S(2)}) async-start(), calls=%async_computation.6 | async-start | bytes 152638464 | tf_op jit(solution)/shard_map/all_gather | solution.py:229
  (136 other events, 601.1 us)
Sparse Core Ops, SparseCore 0:
  13.6 137.6 all-reduce.3
  1306.0 742.9 all-gather.3
